TPU v7x, 32 devices: a whole 2x2x4 slice. The times are simulated.
32 devices in a mesh: segment: 2 (over x), seq: 4 (over y, core), head: 4 (over z).
Axes of the slice: x: 2, y: 2, z: 4, core: 2. Of those that a mesh axis runs over, the one named last changes fastest.
Arguments:
- stream: bfloat16 [2, 512, 4096], P(None, 'seq', 'head'), may hold values from -6 to 6
- in_gain: float32 [2, 4096], P('segment'), may hold values from 0.25 to 1.75
- w_qkv: bfloat16 [2, 4096, 4, 3, 512], P('segment', None, 'head'), may hold values from -0.09375 to 0.09375
- qk_gain: float32 [2, 4, 2, 512], P('segment', 'head'), may hold values from 0.25 to 1.75
- w_one: bfloat16 [2, 4, 512, 768], P('segment', 'head'), may hold values from -0.25 to 0.25
- w_three: bfloat16 [2, 4, 512, 768], P('segment', 'head'), may hold values from -0.25 to 0.25
- w_two: bfloat16 [2, 4, 768, 512], P('segment', 'head'), may hold values from -0.21875 to 0.21875
- token_rate: float32 [2, 2, 512], P('segment', None, 'seq'), may hold values from 0.05 to 1
- out_gain: float32 [2, 4, 512], P('segment', 'head'), may hold values from 0.25 to 1.75
- w_out: bfloat16 [2, 4, 512, 4096], P('segment', 'head'), may hold values from -0.125 to 0.125
Outputs:
- sections_out: bfloat16 [2, 2, 512, 4096], P('segment', None, 'seq', 'head')
All inputs are finite; a program needn't handle non-finite values.
Results may differ from a plain program's by a relative error of at most 0.038.
Values may be sent and summed in bfloat16 or wider, within the bound.
A program may use at most 128 MiB of HBM per device.

v0:
```python
import jax
import jax.numpy as jnp
from jax import lax
from jax.sharding import PartitionSpec as P

NS_STEPS = 2
ns_first = 3.4445
ns_second = -4.775
ns_third = 2.0315
update_step = 1.0
norm_eps = 1e-06
grad_eps = 1e-07


def shifted(array, axis, by):
    devices = lax.axis_size(axis)
    pairs = [(i, i + by) for i in range(devices) if 0 <= i + by < devices]
    return lax.ppermute(array, axis, pairs)


def rms_scale(values):
    return values * lax.rsqrt(jnp.mean(values * values, axis=-1, keepdims=True) + norm_eps)


def contract_rows(left, right):
    return lax.dot_general(
        left, right, (((0,), (0,)), ((), ())), preferred_element_type=jnp.float32
    )


def renormalize(weights, target_norms):
    return weights * (target_norms / (jnp.sqrt(jnp.sum(weights * weights, axis=0)) + norm_eps))


def orthogonal_updates(shares):
    squares = jnp.stack([jnp.sum(share * share) for share in shares])
    totals = lax.psum(squares, "seq")
    current = [
        (shares[index] / (jnp.sqrt(totals[index]) + grad_eps)).astype(jnp.bfloat16)
        for index in range(3)
    ]
    for sweep_index in range(NS_STEPS):
        partial_grams = jnp.stack(
            [
                lax.dot_general(
                    block, block, (((1,), (1,)), ((), ())), preferred_element_type=jnp.float32
                )
                .astype(jnp.bfloat16)
                .astype(jnp.float32)
                for block in current
            ]
        )
        grams = lax.psum(partial_grams.astype(jnp.bfloat16), "seq")
        following = []
        for index in range(3):
            gram_matrix = grams[index]
            square = jnp.dot(gram_matrix, gram_matrix, preferred_element_type=jnp.float32)
            mixing = (ns_second * gram_matrix.astype(jnp.float32) + ns_third * square).astype(
                jnp.bfloat16
            )
            block = current[index]
            following.append(
                (
                    ns_first * block.astype(jnp.float32)
                    + jnp.dot(mixing, block, preferred_element_type=jnp.float32)
                ).astype(jnp.bfloat16)
            )
        current = following
    return (
        lax.all_gather(current[0], "seq", axis=1, tiled=True),
        lax.all_gather(current[1], "seq", axis=1, tiled=True),
        lax.all_gather(current[2], "seq", axis=1, tiled=True),
    )


def run_section(
    residual, gain_row, qkv_matrix, head_gains, rate_row, out_gain_row, out_weights, fasts, norms
):
    values = residual.astype(jnp.float32)
    head_width = head_gains.shape[-1]
    whole = lax.all_gather(residual, "head", axis=1, tiled=True)
    normed = (rms_scale(whole.astype(jnp.float32)) * gain_row).astype(jnp.bfloat16)
    projected = jnp.dot(normed, qkv_matrix, preferred_element_type=jnp.float32)
    projected = projected.reshape(residual.shape[0], 3, head_width)
    queries = rms_scale(projected[:, 0]) * head_gains[0]
    key_rows = (rms_scale(projected[:, 1]) * head_gains[1]).astype(jnp.bfloat16)
    out_grad = (-rate_row[:, None] * projected[:, 2]).astype(jnp.bfloat16)
    gate_fast, up_fast, down_fast = fasts
    gate_low = gate_fast.astype(jnp.bfloat16)
    up_low = up_fast.astype(jnp.bfloat16)
    down_low = down_fast.astype(jnp.bfloat16)
    pre_gate = jnp.dot(key_rows, gate_low, preferred_element_type=jnp.float32)
    pre_up = jnp.dot(key_rows, up_low, preferred_element_type=jnp.float32)
    sigmoid_gate = jax.nn.sigmoid(pre_gate)
    gated = pre_gate * sigmoid_gate
    hidden = (gated * pre_up).astype(jnp.bfloat16)
    backward = lax.dot_general(
        out_grad, down_low, (((1,), (1,)), ((), ())), preferred_element_type=jnp.float32
    )
    grad_gate = (backward * pre_up * sigmoid_gate * (1.0 + pre_gate * (1.0 - sigmoid_gate))).astype(
        jnp.bfloat16
    )
    grad_up = (backward * gated).astype(jnp.bfloat16)
    all_keys, all_grads = (
        lax.all_gather(key_rows, "seq", axis=0, tiled=True),
        lax.all_gather(out_grad, "seq", axis=0, tiled=True),
    )
    hidden_part, gate_part, up_part = (
        lax.all_to_all(hidden, "seq", split_axis=1, concat_axis=0, tiled=True),
        lax.all_to_all(grad_gate, "seq", split_axis=1, concat_axis=0, tiled=True),
        lax.all_to_all(grad_up, "seq", split_axis=1, concat_axis=0, tiled=True),
    )
    shares = (
        contract_rows(all_keys, gate_part),
        contract_rows(all_keys, up_part),
        contract_rows(all_grads, hidden_part),
    )
    gate_step, up_step, down_step = orthogonal_updates(shares)
    gate_fast = renormalize(gate_fast - update_step * gate_step.astype(jnp.float32), norms[0])
    up_fast = renormalize(up_fast - update_step * up_step.astype(jnp.float32), norms[1])
    down_fast = renormalize(down_fast - update_step * down_step.astype(jnp.float32).T, norms[2])
    gate_out = jnp.dot(queries, gate_fast, precision=lax.Precision.HIGHEST)
    up_out = jnp.dot(queries, up_fast, precision=lax.Precision.HIGHEST)
    output = jnp.dot(jax.nn.silu(gate_out) * up_out, down_fast, precision=lax.Precision.HIGHEST)
    normed_out = (rms_scale(output) * out_gain_row).astype(jnp.bfloat16)
    head_terms = jnp.dot(normed_out, out_weights, preferred_element_type=jnp.float32)
    delta = lax.psum_scatter(
        head_terms.astype(jnp.bfloat16), "head", scatter_dimension=1, tiled=True
    ).astype(jnp.float32)
    return ((values + delta).astype(jnp.bfloat16), (gate_fast, up_fast, down_fast))


def shards(stream, in_gain, w_qkv, qk_gain, w_one, w_three, w_two, token_rate, out_gain, w_out):
    segment_index = lax.axis_index("segment")
    span_count = stream.shape[0]
    moments = span_count + lax.axis_size("segment") - 1
    qkv_matrix = w_qkv[0].reshape(w_qkv.shape[1], -1)
    fasts = (
        w_one[0, 0].astype(jnp.float32),
        w_three[0, 0].astype(jnp.float32),
        w_two[0, 0].astype(jnp.float32),
    )
    norms = tuple((jnp.sqrt(jnp.sum(matrix * matrix, axis=0)) for matrix in fasts))
    received = jnp.zeros_like(stream[0])
    collected = jnp.zeros(stream.shape, jnp.bfloat16)
    for moment in range(moments):
        span_index = moment - segment_index
        active = (span_index >= 0) & (span_index < span_count)
        clipped = jnp.clip(span_index, 0, span_count - 1)
        source = jnp.where(segment_index == 0, stream[min(moment, span_count - 1)], received)
        rate_row = lax.dynamic_index_in_dim(token_rate[0], clipped, 0, keepdims=False)
        result, updated = run_section(
            source,
            in_gain[0],
            qkv_matrix,
            qk_gain[0, 0],
            rate_row,
            out_gain[0, 0],
            w_out[0, 0],
            fasts,
            norms,
        )
        fasts = tuple((jnp.where(active, fresh, former) for fresh, former in zip(updated, fasts)))
        chosen = jnp.arange(span_count) == span_index
        collected = jnp.where(chosen[:, None, None], result[None], collected)
        if moment + 1 < moments:
            received = shifted(result, "segment", 1)
    return collected[None]


def solution(mesh):
    placed = (
        P(None, "seq", "head"),
        P("segment", None),
        P("segment", None, "head", None, None),
        P("segment", "head", None, None),
        P("segment", "head", None, None),
        P("segment", "head", None, None),
        P("segment", "head", None, None),
        P("segment", None, "seq"),
        P("segment", "head", None),
        P("segment", "head", None, None),
    )
    return jax.shard_map(
        shards,
        mesh=mesh,
        in_specs=placed,
        out_specs=P("segment", None, "seq", "head"),
        check_vma=False,
    )
```

profile of v0, /device:TPU:0, one launch (start us, length us, event | category | flops | bytes accessed | tf_op | source)
XLA Modules:
  0.0 861.6 jit_solution(11526859129735552482)
XLA Ops:
  8.3 17.0 %copy.13 = bf16[1,4096,1,3,512]{1,4,3,2,0:T(8,128)(2,1)} copy(bf16[1,4096,1,3,512]{4,1,3,2,0:T(8,128)(2,1)} %param.12) | data formatting | bytes 25165824 | tf_op args[2]
  26.4 13.3 %all-gather.9.cloned.1.call-done = bf16[1,128,4096]{2,1,0:T(8,128)(2,1)} async-done(((bf16[1,128,1024]{2,1,0:T(8,128)(2,1)}), bf16[1,128,4096]{2,1,0:T(8,128)(2,1)}) %all-gather.9.cloned.1.call-update) | async-done | bytes 1048592 | tf_op jit(solution)/shard_map/all_gather | solution.py:81
  41.3 8.9 %fusion.4 = f32[128,3,512]{2,0,1:T(8,128)S(1)} fusion(bf16[1,4096,1,3,512]{1,4,3,2,0:T(8,128)(2,1)} %copy.13, bf16[1,128,4096]{2,1,0:T(8,128)(2,1)S(1)} %copy-done.31, f32[4096]{0:T(1024)S(1)} %bitcast.605, f32[128]{0:T(128)S(1)} %add_rsqrt_fusion.11), kind=kOutput, calls=%fused_computation.4 | convolution fusion | flops 1612709888 | bytes 14434816 | tf_op jit(solution)/shard_map/dot_general | solution.py:83
  58.3 8.9 %all_gather.55 = bf16[512,512]{1,0:T(8,128)(2,1)S(1)} all-gather(bf16[128,512]{1,0:T(8,128)(2,1)S(1)} %get-tuple-element.30), channel_id=1, replica_groups=mesh['segment'=2,'seq'=4,'head'=4] {'seq'}, dimensions={0}, use_global_device_ids=true | all-gather | bytes 655360 | tf_op jit(solution)/shard_map/all_gather | solution.py:105
  68.9 7.3 all_gather.56
  76.1 3.4 all-to-all-start.1
  80.5 4.3 all-to-all-done.1
  84.8 3.4 all-to-all-start.2
  89.2 4.2 all-to-all-done.2
  97.0 5.7 psum.63
  108.2 41.7 %all-reduce.7.cloned.1.call-done = bf16[3,512,512]{2,1,0:T(8,128)(2,1)} async-done(((bf16[3,512,512]{2,1,0:T(8,128)(2,1)}), bf16[3,512,512]{2,1,0:T(8,128)(2,1)}) %all-reduce.7.cloned.1.call-update) | async-done | bytes 1572880 | tf_op jit(solution)/shard_map/psum | solution.py:53
  162.1 39.8 %all-reduce.9.cloned.1.call-done = bf16[3,512,512]{2,1,0:T(8,128)(2,1)} async-done(((bf16[3,512,512]{2,1,0:T(8,128)(2,1)}), bf16[3,512,512]{2,1,0:T(8,128)(2,1)}) %all-reduce.9.cloned.1.call-update) | async-done | bytes 1572880 | tf_op jit(solution)/shard_map/psum | solution.py:53
  204.0 8.3 all_gather.59
  215.4 8.7 %all_gather.57 = bf16[512,768]{0,1:T(8,128)(2,1)S(1)} all-gather(bf16[512,192]{0,1:T(8,128)(2,1)S(1)} %fusion.155), channel_id=1, replica_groups=mesh['segment'=2,'seq'=4,'head'=4] {'seq'}, dimensions={1}, use_global_device_ids=true | all-gather | bytes 983040 | tf_op jit(solution)/shard_map/all_gather | solution.py:70
  226.4 8.8 %all_gather.58 = bf16[512,768]{0,1:T(8,128)(2,1)S(1)} all-gather(bf16[512,192]{0,1:T(8,128)(2,1)S(1)} %fusion.154), channel_id=1, replica_groups=mesh['segment'=2,'seq'=4,'head'=4] {'seq'}, dimensions={1}, use_global_device_ids=true | all-gather | bytes 983040 | tf_op jit(solution)/shard_map/all_gather | solution.py:71
  244.5 27.9 %reduce-scatter.4.cloned.1.call-done = bf16[128,1024]{1,0:T(8,128)(2,1)} async-done(((bf16[128,4096]{1,0:T(8,128)(2,1)}), bf16[128,1024]{1,0:T(8,128)(2,1)}) %reduce-scatter.4.cloned.1.call-update) | async-done | bytes 262160 | tf_op jit(solution)/shard_map/reduce_scatter | solution.py:127
  274.2 3.4 collective-permute-start
  277.6 5.1 collective-permute-done
  284.4 28.0 %all-gather.5.cloned.1.call-done = bf16[128,4096]{1,0:T(8,128)(2,1)} async-done(((bf16[128,1024]{1,0:T(8,128)(2,1)}), bf16[128,4096]{1,0:T(8,128)(2,1)}) %all-gather.5.cloned.1.call-update) | async-done | bytes 1048592 | tf_op jit(solution)/shard_map/all_gather | solution.py:81
  314.1 8.9 %fusion.2 = f32[128,3,512]{2,0,1:T(8,128)S(1)} fusion(bf16[1,4096,1,3,512]{1,4,3,2,0:T(8,128)(2,1)} %copy.13, bf16[128,4096]{1,0:T(8,128)(2,1)S(1)} %copy-done.33, f32[128]{0:T(128)S(1)} %add_rsqrt_fusion.7, f32[4096]{0:T(1024)S(1)} %bitcast.606), kind=kOutput, calls=%fused_computation.2 | convolution fusion | flops 1612709888 | bytes 14434816 | tf_op jit(solution)/shard_map/dot_general | solution.py:83
  323.7 8.0 all_gather.61
  335.2 3.4 all-to-all-start.3
  342.0 8.1 all_gather.62
  350.1 3.4 all-to-all-start.4
  358.8 3.4 all-to-all-start.5
  372.7 6.4 psum.66
  386.1 41.7 %all-reduce.11.cloned.1.call-done = bf16[3,512,512]{2,1,0:T(8,128)(2,1)} async-done(((bf16[3,512,512]{2,1,0:T(8,128)(2,1)}), bf16[3,512,512]{2,1,0:T(8,128)(2,1)}) %all-reduce.11.cloned.1.call-update) | async-done | bytes 1572880 | tf_op jit(solution)/shard_map/psum | solution.py:53
  441.9 41.9 %all-reduce.13.cloned.1.call-done = bf16[3,512,512]{2,1,0:T(8,128)(2,1)} async-done(((bf16[3,512,512]{2,1,0:T(8,128)(2,1)}), bf16[3,512,512]{2,1,0:T(8,128)(2,1)}) %all-reduce.13.cloned.1.call-update) | async-done | bytes 1572880 | tf_op jit(solution)/shard_map/psum | solution.py:53
  486.8 8.4 all_gather.65
  500.8 9.0 %all_gather.63 = bf16[512,768]{0,1:T(8,128)(2,1)S(1)} all-gather(bf16[512,192]{0,1:T(8,128)(2,1)} %fusion.149), channel_id=1, replica_groups=mesh['segment'=2,'seq'=4,'head'=4] {'seq'}, dimensions={1}, use_global_device_ids=true | all-gather | bytes 983040 | tf_op jit(solution)/shard_map/all_gather | solution.py:70
  515.2 9.0 %all_gather.64 = bf16[512,768]{0,1:T(8,128)(2,1)S(1)} all-gather(bf16[512,192]{0,1:T(8,128)(2,1)S(1)} %fusion.148), channel_id=1, replica_groups=mesh['segment'=2,'seq'=4,'head'=4] {'seq'}, dimensions={1}, use_global_device_ids=true | all-gather | bytes 983040 | tf_op jit(solution)/shard_map/all_gather | solution.py:71
  534.4 27.9 %reduce-scatter.6.cloned.1.call-done = bf16[128,1024]{1,0:T(8,128)(2,1)} async-done(((bf16[128,4096]{1,0:T(8,128)(2,1)}), bf16[128,1024]{1,0:T(8,128)(2,1)}) %reduce-scatter.6.cloned.1.call-update) | async-done | bytes 262160 | tf_op jit(solution)/shard_map/reduce_scatter | solution.py:127
  564.0 3.4 collective-permute-start.1
  567.4 5.1 collective-permute-done.1
  574.3 28.0 %all-gather.7.cloned.1.call-done = bf16[128,4096]{1,0:T(8,128)(2,1)} async-done(((bf16[128,1024]{1,0:T(8,128)(2,1)}), bf16[128,4096]{1,0:T(8,128)(2,1)}) %all-gather.7.cloned.1.call-update) | async-done | bytes 1048592 | tf_op jit(solution)/shard_map/all_gather | solution.py:81
  603.9 9.0 %fusion = f32[128,3,512]{2,0,1:T(8,128)S(1)} fusion(bf16[1,4096,1,3,512]{1,4,3,2,0:T(8,128)(2,1)} %copy.13, bf16[128,4096]{1,0:T(8,128)(2,1)S(1)} %copy-done.32, f32[128]{0:T(128)S(1)} %add_rsqrt_fusion.3, f32[4096]{0:T(1024)S(1)} %bitcast.607), kind=kOutput, calls=%fused_computation | convolution fusion | flops 1612709888 | bytes 14434816 | tf_op jit(solution)/shard_map/dot_general | solution.py:83
  613.2 7.9 all_gather.67
  625.9 3.4 all-to-all-start.6
  632.8 8.1 all_gather.68
  640.9 3.4 all-to-all-start.7
  649.5 3.4 all-to-all-start.8
  662.9 5.7 psum.69
  674.9 41.7 %all-reduce.15.cloned.1.call-done = bf16[3,512,512]{2,1,0:T(8,128)(2,1)} async-done(((bf16[3,512,512]{2,1,0:T(8,128)(2,1)}), bf16[3,512,512]{2,1,0:T(8,128)(2,1)}) %all-reduce.15.cloned.1.call-update) | async-done | bytes 1572880 | tf_op jit(solution)/shard_map/psum | solution.py:53
  730.1 42.4 %all-reduce.17.cloned.1.call-done = bf16[3,512,512]{2,1,0:T(8,128)(2,1)} async-done(((bf16[3,512,512]{2,1,0:T(8,128)(2,1)}), bf16[3,512,512]{2,1,0:T(8,128)(2,1)}) %all-reduce.17.cloned.1.call-update) | async-done | bytes 1572880 | tf_op jit(solution)/shard_map/psum | solution.py:53
  775.5 8.3 all_gather.71
  789.4 8.9 %all_gather.69 = bf16[512,768]{0,1:T(8,128)(2,1)S(1)} all-gather(bf16[512,192]{0,1:T(8,128)(2,1)} %fusion.143), channel_id=1, replica_groups=mesh['segment'=2,'seq'=4,'head'=4] {'seq'}, dimensions={1}, use_global_device_ids=true | all-gather | bytes 983040 | tf_op jit(solution)/shard_map/all_gather | solution.py:70
  803.6 9.0 %all_gather.70 = bf16[512,768]{0,1:T(8,128)(2,1)S(1)} all-gather(bf16[512,192]{0,1:T(8,128)(2,1)S(1)} %fusion.142), channel_id=1, replica_groups=mesh['segment'=2,'seq'=4,'head'=4] {'seq'}, dimensions={1}, use_global_device_ids=true | all-gather | bytes 983040 | tf_op jit(solution)/shard_map/all_gather | solution.py:71
  824.4 27.9 %reduce-scatter.8.cloned.1.call-done = bf16[128,1024]{1,0:T(8,128)(2,1)} async-done(((bf16[128,4096]{1,0:T(8,128)(2,1)}), bf16[128,1024]{1,0:T(8,128)(2,1)}) %reduce-scatter.8.cloned.1.call-update) | async-done | bytes 262160 | tf_op jit(solution)/shard_map/reduce_scatter | solution.py:127
  (375 shorter events, 196.9 us)
Async XLA Ops:
  6.5 33.1 %all-gather.9.cloned.1.call-start = ((), (), s32[]{:S(2)}) async-start(), calls=%async_computation.23 | async-start | bytes 1310720 | tf_op jit(solution)/shard_map/all_gather | solution.py:81
  8.2 17.0 %copy-start.94 = (f32[1,2,128]{2,1,0:T(2,128)S(1)}, f32[1,2,128]{2,1,0:T(2,128)}, u32[]{:S(2)}) copy-start(f32[1,2,128]{2,1,0:T(2,128)} %param.17) | copy-start | bytes 3076
  8.3 17.5 %copy-start.93 = (f32[1,1,2,512]{3,2,1,0:T(2,128)S(1)}, f32[1,1,2,512]{3,2,1,0:T(2,128)}, u32[]{:S(2)}) copy-start(f32[1,1,2,512]{3,2,1,0:T(2,128)} %param.13) | copy-start | bytes 12292
  8.3 33.0 %copy-start.57 = (f32[1,4096]{1,0:T(1,128)S(1)}, f32[1,4096]{1,0:T(1,128)}, u32[]{:S(2)}) copy-start(f32[1,4096]{1,0:T(1,128)} %param.11) | copy-start | bytes 49156
  26.4 25.7 %copy-start.67 = (f32[1,1,1,512]{3,2,1,0:T(1,128)}, f32[1,1,1,512]{3,2,1,0:T(1,128)S(1)}, u32[]{:S(2)}) copy-start(f32[1,1,1,512]{3,2,1,0:T(1,128)S(1)} %get-tuple-element.33) | copy-start | bytes 6148
  54.9 21.2 %all-to-all-start = ((bf16[128,4,192]{0,2,1:T(8,128)(2,1)}), bf16[128,4,192]{0,2,1:T(8,128)(2,1)S(1)}, u32[]{:S(2)}, u32[]{:S(2)}) async-start(bf16[128,4,192]{0,2,1:T(8,128)(2,1)} %bitcast.19), calls=%async_computation | async-start | bytes 393216 | tf_op jit(solution)/shard_map/all_to_all | solution.py:110
  76.1 8.6 %all-to-all-start.1 = ((bf16[128,4,192]{0,2,1:T(8,128)(2,1)}), bf16[128,4,192]{0,2,1:T(8,128)(2,1)S(1)}, u32[]{:S(2)}, u32[]{:S(2)}) async-start(bf16[128,4,192]{0,2,1:T(8,128)(2,1)} %bitcast.22), calls=%async_computation.1 | async-start | bytes 393216 | tf_op jit(solution)/shard_map/all_to_all | solution.py:111
  84.8 8.6 %all-to-all-start.2 = ((bf16[128,4,192]{0,2,1:T(8,128)(2,1)}), bf16[128,4,192]{0,2,1:T(8,128)(2,1)S(1)}, u32[]{:S(2)}, u32[]{:S(2)}) async-start(bf16[128,4,192]{0,2,1:T(8,128)(2,1)} %bitcast.26), calls=%async_computation.2 | async-start | bytes 393216 | tf_op jit(solution)/shard_map/all_to_all | solution.py:109
  88.2 61.7 %all-reduce.7.cloned.1.call-start = ((), (), s32[]{:S(2)}) async-start(), calls=%async_computation.12 | async-start | bytes 3145728 | tf_op jit(solution)/shard_map/psum | solution.py:53
  89.2 17.0 %copy-start.50 = (f32[512,192]{0,1:T(8,128)}, f32[512,192]{0,1:T(8,128)S(1)}, u32[]{:S(2)}) copy-start(f32[512,192]{0,1:T(8,128)S(1)} %get-tuple-element.49) | copy-start | bytes 1179652
  108.2 44.2 %copy-start.55 = (f32[512,192]{0,1:T(8,128)S(1)}, f32[512,192]{0,1:T(8,128)}, u32[]{:S(2)}) copy-start(f32[512,192]{0,1:T(8,128)} %get-tuple-element.47) | copy-start | bytes 1179652
  108.2 93.7 %all-reduce.9.cloned.1.call-start = ((), (), s32[]{:S(2)}) async-start(), calls=%async_computation.13 | async-start | bytes 3145728 | tf_op jit(solution)/shard_map/psum | solution.py:53
  158.8 113.6 %reduce-scatter.4.cloned.1.call-start = ((), (), s32[]{:S(2)}) async-start(), calls=%async_computation.14 | async-start | bytes 1310720 | tf_op jit(solution)/shard_map/reduce_scatter | solution.py:127
  236.0 96.4 %copy-start.75 = (f32[512]{0:T(512)}, f32[512]{0:T(512)S(1)}, u32[]{:S(2)}) copy-start(f32[512]{0:T(512)S(1)} %add_divide_fusion.11) | copy-start | bytes 6148
  237.1 95.8 %copy-start.58 = (f32[768]{0:T(1024)}, f32[768]{0:T(1024)S(1)}, u32[]{:S(2)}) copy-start(f32[768]{0:T(1024)S(1)} %add_divide_fusion.8) | copy-start | bytes 9220
  237.5 94.2 %copy-start.70 = (f32[768]{0:T(1024)}, f32[768]{0:T(1024)S(1)}, u32[]{:S(2)}) copy-start(f32[768]{0:T(1024)S(1)} %add_divide_fusion.7) | copy-start | bytes 9220
  244.5 67.9 %all-gather.5.cloned.1.call-start = ((), (), s32[]{:S(2)}) async-start(), calls=%async_computation.15 | async-start | bytes 1310720 | tf_op jit(solution)/shard_map/all_gather | solution.py:81
  274.2 8.5 collective-permute-start
  335.2 15.0 %all-to-all-start.3 = ((bf16[128,4,192]{0,2,1:T(8,128)(2,1)}), bf16[128,4,192]{0,2,1:T(8,128)(2,1)S(1)}, u32[]{:S(2)}, u32[]{:S(2)}) async-start(bf16[128,4,192]{0,2,1:T(8,128)(2,1)} %bitcast.54), calls=%async_computation.4 | async-start | bytes 393216 | tf_op jit(solution)/shard_map/all_to_all | solution.py:110
  350.1 8.6 %all-to-all-start.4 = ((bf16[128,4,192]{0,2,1:T(8,128)(2,1)}), bf16[128,4,192]{0,2,1:T(8,128)(2,1)S(1)}, u32[]{:S(2)}, u32[]{:S(2)}) async-start(bf16[128,4,192]{0,2,1:T(8,128)(2,1)} %bitcast.57), calls=%async_computation.5 | async-start | bytes 393216 | tf_op jit(solution)/shard_map/all_to_all | solution.py:111
  358.8 8.6 %all-to-all-start.5 = ((bf16[128,4,192]{0,2,1:T(8,128)(2,1)}), bf16[128,4,192]{0,2,1:T(8,128)(2,1)S(1)}, u32[]{:S(2)}, u32[]{:S(2)}) async-start(bf16[128,4,192]{0,2,1:T(8,128)(2,1)} %bitcast.60), calls=%async_computation.6 | async-start | bytes 393216 | tf_op jit(solution)/shard_map/all_to_all | solution.py:109
  362.2 65.6 %all-reduce.11.cloned.1.call-start = ((), (), s32[]{:S(2)}) async-start(), calls=%async_computation.16 | async-start | bytes 3145728 | tf_op jit(solution)/shard_map/psum | solution.py:53
  370.1 13.9 %copy-start.52 = (f32[512,192]{0,1:T(8,128)S(1)}, f32[512,192]{0,1:T(8,128)}, u32[]{:S(2)}) copy-start(f32[512,192]{0,1:T(8,128)} %get-tuple-element.57) | copy-start | bytes 1179652
  386.1 97.8 %all-reduce.13.cloned.1.call-start = ((), (), s32[]{:S(2)}) async-start(), calls=%async_computation.17 | async-start | bytes 3145728 | tf_op jit(solution)/shard_map/psum | solution.py:53
  440.8 121.5 %reduce-scatter.6.cloned.1.call-start = ((), (), s32[]{:S(2)}) async-start(), calls=%async_computation.18 | async-start | bytes 1310720 | tf_op jit(solution)/shard_map/reduce_scatter | solution.py:127
  515.1 11.6 %copy-start.24 = (bf16[512,768]{0,1:T(8,128)(2,1)S(1)}, bf16[512,768]{0,1:T(8,128)(2,1)}, u32[]{:S(2)}) copy-start(bf16[512,768]{0,1:T(8,128)(2,1)} %copy-done.23) | copy-start | bytes 2359300
  515.1 11.6 %copy-start.30 = (f32[128,3,512]{2,0,1:T(8,128)S(1)}, f32[128,3,512]{2,0,1:T(8,128)}, u32[]{:S(2)}) copy-start(f32[128,3,512]{2,0,1:T(8,128)} %copy-done.29) | copy-start | bytes 2359300
  515.1 11.6 %copy-start.59 = (f32[768]{0:T(1024)S(1)}, f32[768]{0:T(1024)}, u32[]{:S(2)}) copy-start(f32[768]{0:T(1024)} %copy-done.58) | copy-start | bytes 9220
  515.2 11.6 %copy-start.83 = (f32[768]{0:T(1024)S(1)}, f32[768]{0:T(1024)}, u32[]{:S(2)}) copy-start(f32[768]{0:T(1024)} %add_divide_fusion.6) | copy-start | bytes 9220
  526.8 94.4 %copy-start.81 = (f32[768]{0:T(1024)}, f32[768]{0:T(1024)S(1)}, u32[]{:S(2)}) copy-start(f32[768]{0:T(1024)S(1)} %add_divide_fusion.5) | copy-start | bytes 9220
  532.6 29.7 %copy-start.41 = (bf16[128,1024]{1,0:T(8,128)(2,1)S(1)}, bf16[128,1024]{1,0:T(8,128)(2,1)}, u32[]{:S(2)}) copy-start(bf16[128,1024]{1,0:T(8,128)(2,1)} %bitcast_select_fusion.1) | copy-start | bytes 786436
  534.4 67.9 %all-gather.7.cloned.1.call-start = ((), (), s32[]{:S(2)}) async-start(), calls=%async_computation.19 | async-start | bytes 1310720 | tf_op jit(solution)/shard_map/all_gather | solution.py:81
  564.0 8.5 collective-permute-start.1
  603.9 17.2 %copy-start.21 = (bf16[512,768]{0,1:T(8,128)(2,1)S(1)}, bf16[512,768]{0,1:T(8,128)(2,1)}, u32[]{:S(2)}) copy-start(bf16[512,768]{0,1:T(8,128)(2,1)} %copy-done.20) | copy-start | bytes 2359300
  625.9 15.0 %all-to-all-start.6 = ((bf16[128,4,192]{0,2,1:T(8,128)(2,1)}), bf16[128,4,192]{0,2,1:T(8,128)(2,1)S(1)}, u32[]{:S(2)}, u32[]{:S(2)}) async-start(bf16[128,4,192]{0,2,1:T(8,128)(2,1)} %bitcast.84), calls=%async_computation.8 | async-start | bytes 393216 | tf_op jit(solution)/shard_map/all_to_all | solution.py:110
  640.9 8.6 %all-to-all-start.7 = ((bf16[128,4,192]{0,2,1:T(8,128)(2,1)}), bf16[128,4,192]{0,2,1:T(8,128)(2,1)S(1)}, u32[]{:S(2)}, u32[]{:S(2)}) async-start(bf16[128,4,192]{0,2,1:T(8,128)(2,1)} %bitcast.87), calls=%async_computation.9 | async-start | bytes 393216 | tf_op jit(solution)/shard_map/all_to_all | solution.py:111
  649.5 8.6 %all-to-all-start.8 = ((bf16[128,4,192]{0,2,1:T(8,128)(2,1)}), bf16[128,4,192]{0,2,1:T(8,128)(2,1)S(1)}, u32[]{:S(2)}, u32[]{:S(2)}) async-start(bf16[128,4,192]{0,2,1:T(8,128)(2,1)} %bitcast.90), calls=%async_computation.10 | async-start | bytes 393216 | tf_op jit(solution)/shard_map/all_to_all | solution.py:109
  652.9 63.6 %all-reduce.15.cloned.1.call-start = ((), (), s32[]{:S(2)}) async-start(), calls=%async_computation.20 | async-start | bytes 3145728 | tf_op jit(solution)/shard_map/psum | solution.py:53
  660.9 11.9 %copy-start.49 = (f32[512,192]{0,1:T(8,128)S(1)}, f32[512,192]{0,1:T(8,128)}, u32[]{:S(2)}) copy-start(f32[512,192]{0,1:T(8,128)} %get-tuple-element.65) | copy-start | bytes 1179652
  674.8 97.7 %all-reduce.17.cloned.1.call-start = ((), (), s32[]{:S(2)}) async-start(), calls=%async_computation.21 | async-start | bytes 3145728 | tf_op jit(solution)/shard_map/psum | solution.py:53
  729.5 122.8 %reduce-scatter.8.cloned.1.call-start = ((), (), s32[]{:S(2)}) async-start(), calls=%async_computation.22 | async-start | bytes 1310720 | tf_op jit(solution)/shard_map/reduce_scatter | solution.py:127
  730.1 53.7 %copy-start.77 = (f32[512]{0:T(512)S(1)}, f32[512]{0:T(512)}, u32[]{:S(2)}) copy-start(f32[512]{0:T(512)} %copy-done.75) | copy-start | bytes 6148
  730.1 53.7 %copy-start.87 = (f32[512]{0:T(512)S(1)}, f32[512]{0:T(512)}, u32[]{:S(2)}) copy-start(f32[512]{0:T(512)} %add_divide_fusion.10) | copy-start | bytes 6148
  786.5 11.7 %copy-start.60 = (f32[768]{0:T(1024)S(1)}, f32[768]{0:T(1024)}, u32[]{:S(2)}) copy-start(f32[768]{0:T(1024)} %copy-done.58) | copy-start | bytes 9220
  786.5 11.7 %copy-start.84 = (f32[768]{0:T(1024)S(1)}, f32[768]{0:T(1024)}, u32[]{:S(2)}) copy-start(f32[768]{0:T(1024)} %add_divide_fusion.6) | copy-start | bytes 9220
  822.5 29.7 %copy-start.40 = (bf16[128,1024]{1,0:T(8,128)(2,1)S(1)}, bf16[128,1024]{1,0:T(8,128)(2,1)}, u32[]{:S(2)}) copy-start(bf16[128,1024]{1,0:T(8,128)(2,1)} %bitcast_select_fusion) | copy-start | bytes 786436
  824.3 29.0 %copy-start.43 = (bf16[128,1024]{1,0:T(8,128)(2,1)S(1)}, bf16[128,1024]{1,0:T(8,128)(2,1)}, u32[]{:S(2)}) copy-start(bf16[128,1024]{1,0:T(8,128)(2,1)} %copy-done.42) | copy-start | bytes 786436
  824.3 29.0 %copy-start.45 = (bf16[128,1024]{1,0:T(8,128)(2,1)S(1)}, bf16[128,1024]{1,0:T(8,128)(2,1)}, u32[]{:S(2)}) copy-start(bf16[128,1024]{1,0:T(8,128)(2,1)} %copy-done.44) | copy-start | bytes 786436
  (77 other events, 311.0 us)
Sparse Core Ops, SparseCore 0:
  8.9 30.6 all-gather.8
  108.3 41.5 all-reduce.6
  158.9 42.9 all-reduce.8
  244.6 27.7 reduce-scatter.3
  284.5 27.8 all-gather.4
  386.2 41.5 all-reduce.10
  440.9 42.9 all-reduce.12
  534.5 27.7 reduce-scatter.5
  574.4 27.8 all-gather.6
  674.9 41.5 all-reduce.14
  729.6 42.8 all-reduce.16
  824.5 27.7 reduce-scatter.7
where the time goes:
time: 873 us; the launch traced here: 862 us
  waiting for transfers between devices  431 us (49%)
  blocking collectives  145 us (17%)
  matrix products  131 us (15%)
  other arithmetic  53 us (6%)
  local copies, waits for them, and re-layouts  42.2 us (5%)
  starting transfers between devices  37.5 us (4%)
  between operations  21.7 us (2%)
    psum x6, waiting for transfers between devices, orthogonal_updates(): grams = lax.psum(partial_grams.astype(jnp.bfloat16), 'seq')  249 us
    reduce_scatter x3, waiting for transfers between devices, run_section(): lax.psum_scatter(head_terms.astype(jnp.bfloat16), 'head', scatter_dimensi...  83.7 us
    all_gather x3, waiting for transfers between devices, run_section(): whole = lax.all_gather(residual, 'head', axis=1, tiled=True)  69.2 us
    dot_general x18, matrix products, orthogonal_updates(): jnp.dot(mixing, block, preferred_element_type=jnp.float32)  43.4 us
    unnamed x207, local copies, waits for them, and re-layouts  27 us
    all_gather x3, blocking collectives, orthogonal_updates(): lax.all_gather(current[1], 'seq', axis=1, tiled=True)  26.8 us
    dot_general x3, matrix products, run_section(): projected = jnp.dot(normed, qkv_matrix, preferred_element_type=jnp.float32)  26.8 us
    all_gather x3, blocking collectives, orthogonal_updates(): lax.all_gather(current[0], 'seq', axis=1, tiled=True)  26.6 us
  transfers between devices with their start and end apart: 23, of which 20 were waited for; matrix products, arithmetic and copies ran while one was open for 5% of the time, Pallas kernels for 0%

commit v1 on v0

--- a/solution.py
+++ b/solution.py
@@ -50,7 +50,9 @@
                 for block in current
             ]
         )
-        grams = lax.psum(partial_grams.astype(jnp.bfloat16), "seq")
+        own = partial_grams.astype(jnp.bfloat16)
+        parts = lax.all_gather(own, "seq")
+        grams = jnp.sum(parts, axis=0)
         following = []
         for index in range(3):
             gram_matrix = grams[index]

time: 873 us -> 901 us (1.032)
  waiting for transfers between devices: 431 us -> 450 us
  other arithmetic: 53 us -> 70.7 us
    all_gather x0 -> x6, waiting for transfers between devices: none -> 270 us  [orthogonal_updates(): parts = lax.all_gather(own, 'seq')]
    psum x6 -> x0, waiting for transfers between devices: 249 us -> none  [orthogonal_updates(): grams = lax.psum(partial_grams.astype(jnp.bfloat16), 'seq')]
    reduce_sum x0 -> x6, other arithmetic: none -> 29.9 us  [orthogonal_updates(): grams = jnp.sum(parts, axis=0)]
    unnamed x207 -> x187, local copies, waits for them, and re-layouts: 27 us -> 22.8 us
where the time goes in v1:
time: 901 us; the launch traced here: 890 us
  waiting for transfers between devices  450 us (50%)
  blocking collectives  145 us (16%)
  matrix products  126 us (14%)
  other arithmetic  70.7 us (8%)
  starting transfers between devices  38.9 us (4%)
  local copies, waits for them, and re-layouts  37.8 us (4%)
  between operations  21.1 us (2%)
    all_gather x6, waiting for transfers between devices, orthogonal_updates(): parts = lax.all_gather(own, 'seq')  270 us
    reduce_scatter x3, waiting for transfers between devices, run_section(): lax.psum_scatter(head_terms.astype(jnp.bfloat16), 'head', scatter_dimensi...  82.2 us
    all_gather x3, waiting for transfers between devices, run_section(): whole = lax.all_gather(residual, 'head', axis=1, tiled=True)  69.2 us
    dot_general x18, matrix products, orthogonal_updates(): jnp.dot(mixing, block, preferred_element_type=jnp.float32)  39.7 us
    reduce_sum x6, other arithmetic, orthogonal_updates(): grams = jnp.sum(parts, axis=0)  29.9 us
    dot_general x3, matrix products, run_section(): projected = jnp.dot(normed, qkv_matrix, preferred_element_type=jnp.float32)  26.8 us
    all_gather x3, blocking collectives, orthogonal_updates(): lax.all_gather(current[2], 'seq', axis=1, tiled=True)  26.7 us
    all_gather x3, blocking collectives, orthogonal_updates(): lax.all_gather(current[1], 'seq', axis=1, tiled=True)  26.5 us
  transfers between devices with their start and end apart: 23, of which 20 were waited for; matrix products, arithmetic and copies ran while one was open for 5% of the time, Pallas kernels for 0%

profile of v1, /device:TPU:0, one launch (start us, length us, event | category | flops | bytes accessed | tf_op | source)
XLA Modules:
  0.0 889.6 jit_solution(12160732989286323918)
XLA Ops:
  8.3 17.0 %copy.34 = bf16[1,4096,1,3,512]{1,4,3,2,0:T(8,128)(2,1)} copy(bf16[1,4096,1,3,512]{4,1,3,2,0:T(8,128)(2,1)} %param.12) | data formatting | bytes 25165824 | tf_op args[2]
  26.4 13.2 %all-gather.27.cloned.1.call-done = bf16[1,128,4096]{2,1,0:T(8,128)(2,1)} async-done(((bf16[1,128,1024]{2,1,0:T(8,128)(2,1)}), bf16[1,128,4096]{2,1,0:T(8,128)(2,1)}) %all-gather.27.cloned.1.call-update) | async-done | bytes 1048592 | tf_op jit(solution)/shard_map/all_gather | solution.py:83
  41.3 8.9 %fusion.4 = f32[128,3,512]{2,0,1:T(8,128)S(1)} fusion(bf16[1,4096,1,3,512]{1,4,3,2,0:T(8,128)(2,1)} %copy.34, bf16[1,128,4096]{2,1,0:T(8,128)(2,1)S(1)} %copy-done.29, f32[4096]{0:T(1024)S(1)} %bitcast.605, f32[128]{0:T(128)S(1)} %add_rsqrt_fusion.11), kind=kOutput, calls=%fused_computation.4 | convolution fusion | flops 1612709888 | bytes 14434816 | tf_op jit(solution)/shard_map/dot_general | solution.py:85
  58.4 8.9 %all_gather.79 = bf16[512,512]{1,0:T(8,128)(2,1)S(1)} all-gather(bf16[128,512]{1,0:T(8,128)(2,1)S(1)} %get-tuple-element.30), channel_id=1, replica_groups=mesh['segment'=2,'seq'=4,'head'=4] {'seq'}, dimensions={0}, use_global_device_ids=true | all-gather | bytes 655360 | tf_op jit(solution)/shard_map/all_gather | solution.py:107
  68.9 7.3 all_gather.80
  80.5 4.4 all-to-all-done.1
  84.9 3.4 all-to-all-start.2
  89.2 4.3 all-to-all-done.2
  96.2 5.7 psum.21
  106.9 45.2 %all-gather.11.cloned.1.call-done = bf16[4,3,512,512]{3,2,1,0:T(8,128)(2,1)} async-done(((bf16[1,3,512,512]{3,2,1,0:T(8,128)(2,1)}), bf16[4,3,512,512]{3,2,1,0:T(8,128)(2,1)}) %all-gather.11.cloned.1.call-update) | async-done | bytes 6291472 | tf_op jit(solution)/shard_map/all_gather | solution.py:54
  152.1 4.1 reduce_sum.375
  165.0 43.4 %all-gather.13.cloned.1.call-done = bf16[4,3,512,512]{3,2,1,0:T(8,128)(2,1)} async-done(((bf16[1,3,512,512]{3,2,1,0:T(8,128)(2,1)}), bf16[4,3,512,512]{3,2,1,0:T(8,128)(2,1)}) %all-gather.13.cloned.1.call-update) | async-done | bytes 6291472 | tf_op jit(solution)/shard_map/all_gather | solution.py:54
  208.4 4.1 reduce_sum.376
  217.0 8.9 %all_gather.85 = bf16[512,768]{0,1:T(8,128)(2,1)S(1)} all-gather(bf16[512,192]{0,1:T(8,128)(2,1)} %fusion.153), channel_id=1, replica_groups=mesh['segment'=2,'seq'=4,'head'=4] {'seq'}, dimensions={1}, use_global_device_ids=true | all-gather | bytes 983040 | tf_op jit(solution)/shard_map/all_gather | solution.py:74
  226.4 8.8 all_gather.83
  235.2 8.7 all_gather.84
  252.3 27.4 %reduce-scatter.4.cloned.1.call-done = bf16[128,1024]{1,0:T(8,128)(2,1)} async-done(((bf16[128,4096]{1,0:T(8,128)(2,1)}), bf16[128,1024]{1,0:T(8,128)(2,1)}) %reduce-scatter.4.cloned.1.call-update) | async-done | bytes 262160 | tf_op jit(solution)/shard_map/reduce_scatter | solution.py:129
  281.5 3.6 collective-permute-start
  285.0 5.0 collective-permute-done
  291.7 28.0 %all-gather.15.cloned.1.call-done = bf16[128,4096]{1,0:T(8,128)(2,1)} async-done(((bf16[128,1024]{1,0:T(8,128)(2,1)}), bf16[128,4096]{1,0:T(8,128)(2,1)}) %all-gather.15.cloned.1.call-update) | async-done | bytes 1048592 | tf_op jit(solution)/shard_map/all_gather | solution.py:83
  321.3 8.9 %fusion.2 = f32[128,3,512]{2,0,1:T(8,128)S(1)} fusion(bf16[1,4096,1,3,512]{1,4,3,2,0:T(8,128)(2,1)} %copy.34, bf16[128,4096]{1,0:T(8,128)(2,1)S(1)} %copy-done.31, f32[128]{0:T(128)S(1)} %add_rsqrt_fusion.7, f32[4096]{0:T(1024)S(1)} %bitcast.606), kind=kOutput, calls=%fused_computation.2 | convolution fusion | flops 1612709888 | bytes 14434816 | tf_op jit(solution)/shard_map/dot_general | solution.py:85
  331.1 7.6 all_gather.87
  348.9 8.1 all_gather.88
  357.0 3.4 all-to-all-start.4
  379.5 6.4 psum.22
  392.8 45.2 %all-gather.17.cloned.1.call-done = bf16[4,3,512,512]{3,2,1,0:T(8,128)(2,1)} async-done(((bf16[1,3,512,512]{3,2,1,0:T(8,128)(2,1)}), bf16[4,3,512,512]{3,2,1,0:T(8,128)(2,1)}) %all-gather.17.cloned.1.call-update) | async-done | bytes 6291472 | tf_op jit(solution)/shard_map/all_gather | solution.py:54
  438.0 5.4 reduce_sum.390
  456.1 45.0 %all-gather.19.cloned.1.call-done = bf16[4,3,512,512]{3,2,1,0:T(8,128)(2,1)} async-done(((bf16[1,3,512,512]{3,2,1,0:T(8,128)(2,1)}), bf16[4,3,512,512]{3,2,1,0:T(8,128)(2,1)}) %all-gather.19.cloned.1.call-update) | async-done | bytes 6291472 | tf_op jit(solution)/shard_map/all_gather | solution.py:54
  501.1 5.4 reduce_sum.391
  514.3 8.9 %all_gather.93 = bf16[512,768]{0,1:T(8,128)(2,1)S(1)} all-gather(bf16[512,192]{0,1:T(8,128)(2,1)} %fusion.147), channel_id=1, replica_groups=mesh['segment'=2,'seq'=4,'head'=4] {'seq'}, dimensions={1}, use_global_device_ids=true | all-gather | bytes 983040 | tf_op jit(solution)/shard_map/all_gather | solution.py:74
  524.5 8.7 all_gather.91
  534.1 8.8 all_gather.92
  551.5 27.4 %reduce-scatter.6.cloned.1.call-done = bf16[128,1024]{1,0:T(8,128)(2,1)} async-done(((bf16[128,4096]{1,0:T(8,128)(2,1)}), bf16[128,1024]{1,0:T(8,128)(2,1)}) %reduce-scatter.6.cloned.1.call-update) | async-done | bytes 262160 | tf_op jit(solution)/shard_map/reduce_scatter | solution.py:129
  580.6 3.8 collective-permute-start.1
  584.4 4.7 collective-permute-done.1
  590.8 28.0 %all-gather.21.cloned.1.call-done = bf16[128,4096]{1,0:T(8,128)(2,1)} async-done(((bf16[128,1024]{1,0:T(8,128)(2,1)}), bf16[128,4096]{1,0:T(8,128)(2,1)}) %all-gather.21.cloned.1.call-update) | async-done | bytes 1048592 | tf_op jit(solution)/shard_map/all_gather | solution.py:83
  620.5 9.0 %fusion = f32[128,3,512]{2,0,1:T(8,128)S(1)} fusion(bf16[1,4096,1,3,512]{1,4,3,2,0:T(8,128)(2,1)} %copy.34, bf16[128,4096]{1,0:T(8,128)(2,1)S(1)} %copy-done.30, f32[128]{0:T(128)S(1)} %add_rsqrt_fusion.3, f32[4096]{0:T(1024)S(1)} %bitcast.607), kind=kOutput, calls=%fused_computation | convolution fusion | flops 1612709888 | bytes 14434816 | tf_op jit(solution)/shard_map/dot_general | solution.py:85
  629.7 7.7 all_gather.95
  649.1 8.1 all_gather.96
  679.3 5.7 psum.23
  691.4 45.0 %all-gather.23.cloned.1.call-done = bf16[4,3,512,512]{3,2,1,0:T(8,128)(2,1)} async-done(((bf16[1,3,512,512]{3,2,1,0:T(8,128)(2,1)}), bf16[4,3,512,512]{3,2,1,0:T(8,128)(2,1)}) %all-gather.23.cloned.1.call-update) | async-done | bytes 6291472 | tf_op jit(solution)/shard_map/all_gather | solution.py:54
  736.4 5.4 reduce_sum.402
  753.5 46.5 %all-gather.25.cloned.1.call-done = bf16[4,3,512,512]{3,2,1,0:T(8,128)(2,1)} async-done(((bf16[1,3,512,512]{3,2,1,0:T(8,128)(2,1)}), bf16[4,3,512,512]{3,2,1,0:T(8,128)(2,1)}) %all-gather.25.cloned.1.call-update) | async-done | bytes 6291472 | tf_op jit(solution)/shard_map/all_gather | solution.py:54
  800.0 5.4 reduce_sum.403
  813.6 8.8 all_gather.101
  824.4 8.7 all_gather.99
  834.3 8.9 %all_gather.100 = bf16[512,768]{0,1:T(8,128)(2,1)S(1)} all-gather(bf16[512,192]{0,1:T(8,128)(2,1)S(1)} %fusion.142), channel_id=1, replica_groups=mesh['segment'=2,'seq'=4,'head'=4] {'seq'}, dimensions={1}, use_global_device_ids=true | all-gather | bytes 983040 | tf_op jit(solution)/shard_map/all_gather | solution.py:73
  853.1 27.4 %reduce-scatter.8.cloned.1.call-done = bf16[128,1024]{1,0:T(8,128)(2,1)} async-done(((bf16[128,4096]{1,0:T(8,128)(2,1)}), bf16[128,1024]{1,0:T(8,128)(2,1)}) %reduce-scatter.8.cloned.1.call-update) | async-done | bytes 262160 | tf_op jit(solution)/shard_map/reduce_scatter | solution.py:129
  (361 shorter events, 195.6 us)
Async XLA Ops:
  6.5 33.1 %all-gather.27.cloned.1.call-start = ((), (), s32[]{:S(2)}) async-start(), calls=%async_computation.23 | async-start | bytes 1310720 | tf_op jit(solution)/shard_map/all_gather | solution.py:83
  8.2 17.0 %copy-start.86 = (f32[1,2,128]{2,1,0:T(2,128)S(1)}, f32[1,2,128]{2,1,0:T(2,128)}, u32[]{:S(2)}) copy-start(f32[1,2,128]{2,1,0:T(2,128)} %param.17) | copy-start | bytes 3076
  8.3 17.6 %copy-start.85 = (f32[1,1,2,512]{3,2,1,0:T(2,128)S(1)}, f32[1,1,2,512]{3,2,1,0:T(2,128)}, u32[]{:S(2)}) copy-start(f32[1,1,2,512]{3,2,1,0:T(2,128)} %param.13) | copy-start | bytes 12292
  8.3 33.0 %copy-start.51 = (f32[1,4096]{1,0:T(1,128)S(1)}, f32[1,4096]{1,0:T(1,128)}, u32[]{:S(2)}) copy-start(f32[1,4096]{1,0:T(1,128)} %param.11) | copy-start | bytes 49156
  26.4 25.6 %copy-start.61 = (f32[1,1,1,512]{3,2,1,0:T(1,128)}, f32[1,1,1,512]{3,2,1,0:T(1,128)S(1)}, u32[]{:S(2)}) copy-start(f32[1,1,1,512]{3,2,1,0:T(1,128)S(1)} %get-tuple-element.33) | copy-start | bytes 6148
  55.0 21.2 %all-to-all-start = ((bf16[128,4,192]{0,2,1:T(8,128)(2,1)}), bf16[128,4,192]{0,2,1:T(8,128)(2,1)S(1)}, u32[]{:S(2)}, u32[]{:S(2)}) async-start(bf16[128,4,192]{0,2,1:T(8,128)(2,1)} %bitcast.19), calls=%async_computation | async-start | bytes 393216 | tf_op jit(solution)/shard_map/all_to_all | solution.py:112
  76.2 8.6 all-to-all-start.1
  84.9 8.6 all-to-all-start.2
  88.2 63.8 %all-gather.11.cloned.1.call-start = ((), (), s32[]{:S(2)}) async-start(), calls=%async_computation.12 | async-start | bytes 7864320 | tf_op jit(solution)/shard_map/all_gather | solution.py:54
  94.4 10.7 %copy-start.46 = (f32[512,192]{0,1:T(8,128)}, f32[512,192]{0,1:T(8,128)S(1)}, u32[]{:S(2)}) copy-start(f32[512,192]{0,1:T(8,128)S(1)} %get-tuple-element.47) | copy-start | bytes 1179652
  106.8 101.6 %all-gather.13.cloned.1.call-start = ((), (), s32[]{:S(2)}) async-start(), calls=%async_computation.13 | async-start | bytes 7864320 | tf_op jit(solution)/shard_map/all_gather | solution.py:54
  161.9 117.8 %reduce-scatter.4.cloned.1.call-start = ((), (), s32[]{:S(2)}) async-start(), calls=%async_computation.14 | async-start | bytes 1310720 | tf_op jit(solution)/shard_map/reduce_scatter | solution.py:129
  226.3 18.0 %copy-start.67 = (f32[512]{0:T(512)}, f32[512]{0:T(512)S(1)}, u32[]{:S(2)}) copy-start(f32[512]{0:T(512)S(1)} %get-tuple-element.9) | copy-start | bytes 6148
  226.3 18.1 %copy-start.4 = (bf16[1,1,512,768]{2,3,1,0:T(8,128)(2,1)S(1)}, bf16[1,1,512,768]{2,3,1,0:T(8,128)(2,1)}, u32[]{:S(2)}) copy-start(bf16[1,1,512,768]{2,3,1,0:T(8,128)(2,1)} %copy.36) | copy-start | bytes 2359300
  243.9 95.4 %copy-start.70 = (f32[512]{0:T(512)}, f32[512]{0:T(512)S(1)}, u32[]{:S(2)}) copy-start(f32[512]{0:T(512)S(1)} %add_divide_fusion.11) | copy-start | bytes 6148
  244.4 95.4 %copy-start.52 = (f32[768]{0:T(1024)}, f32[768]{0:T(1024)S(1)}, u32[]{:S(2)}) copy-start(f32[768]{0:T(1024)S(1)} %add_divide_fusion.8) | copy-start | bytes 9220
  244.9 93.8 %copy-start.64 = (f32[768]{0:T(1024)}, f32[768]{0:T(1024)S(1)}, u32[]{:S(2)}) copy-start(f32[768]{0:T(1024)S(1)} %add_divide_fusion.7) | copy-start | bytes 9220
  252.2 67.5 %all-gather.15.cloned.1.call-start = ((), (), s32[]{:S(2)}) async-start(), calls=%async_computation.15 | async-start | bytes 1310720 | tf_op jit(solution)/shard_map/all_gather | solution.py:83
  281.5 8.5 collective-permute-start
  342.1 14.9 %all-to-all-start.3 = ((bf16[128,4,192]{0,2,1:T(8,128)(2,1)}), bf16[128,4,192]{0,2,1:T(8,128)(2,1)S(1)}, u32[]{:S(2)}, u32[]{:S(2)}) async-start(bf16[128,4,192]{0,2,1:T(8,128)(2,1)} %bitcast.54), calls=%async_computation.4 | async-start | bytes 393216 | tf_op jit(solution)/shard_map/all_to_all | solution.py:112
  357.0 8.6 all-to-all-start.4
  365.7 8.6 all-to-all-start.5
  369.1 68.9 %all-gather.17.cloned.1.call-start = ((), (), s32[]{:S(2)}) async-start(), calls=%async_computation.16 | async-start | bytes 7864320 | tf_op jit(solution)/shard_map/all_gather | solution.py:54
  377.0 13.7 %copy-start.44 = (f32[512,192]{0,1:T(8,128)S(1)}, f32[512,192]{0,1:T(8,128)}, u32[]{:S(2)}) copy-start(f32[512,192]{0,1:T(8,128)} %get-tuple-element.57) | copy-start | bytes 1179652
  392.7 108.4 %all-gather.19.cloned.1.call-start = ((), (), s32[]{:S(2)}) async-start(), calls=%async_computation.17 | async-start | bytes 7864320 | tf_op jit(solution)/shard_map/all_gather | solution.py:54
  454.6 124.3 %reduce-scatter.6.cloned.1.call-start = ((), (), s32[]{:S(2)}) async-start(), calls=%async_computation.18 | async-start | bytes 1310720 | tf_op jit(solution)/shard_map/reduce_scatter | solution.py:129
  523.3 24.9 %copy-start.16 = (bf16[512,768]{0,1:T(8,128)(2,1)}, bf16[512,768]{0,1:T(8,128)(2,1)S(1)}, u32[]{:S(2)}) copy-start(bf16[512,768]{0,1:T(8,128)(2,1)S(1)} %all_gather.93) | copy-start | bytes 2359300
  524.5 113.9 %copy-start.80 = (f32[512]{0:T(512)}, f32[512]{0:T(512)S(1)}, u32[]{:S(2)}) copy-start(f32[512]{0:T(512)S(1)} %add_divide_fusion.10) | copy-start | bytes 6148
  534.1 105.2 %copy-start.78 = (f32[768]{0:T(1024)}, f32[768]{0:T(1024)S(1)}, u32[]{:S(2)}) copy-start(f32[768]{0:T(1024)S(1)} %add_divide_fusion.6) | copy-start | bytes 9220
  543.9 93.6 %copy-start.76 = (f32[768]{0:T(1024)}, f32[768]{0:T(1024)S(1)}, u32[]{:S(2)}) copy-start(f32[768]{0:T(1024)S(1)} %add_divide_fusion.5) | copy-start | bytes 9220
  549.7 29.2 %copy-start.35 = (bf16[128,1024]{1,0:T(8,128)(2,1)S(1)}, bf16[128,1024]{1,0:T(8,128)(2,1)}, u32[]{:S(2)}) copy-start(bf16[128,1024]{1,0:T(8,128)(2,1)} %bitcast_select_fusion.1) | copy-start | bytes 786436
  551.4 67.4 %all-gather.21.cloned.1.call-start = ((), (), s32[]{:S(2)}) async-start(), calls=%async_computation.19 | async-start | bytes 1310720 | tf_op jit(solution)/shard_map/all_gather | solution.py:83
  580.6 8.5 collective-permute-start.1
  620.5 17.0 %copy-start.20 = (bf16[512,768]{0,1:T(8,128)(2,1)S(1)}, bf16[512,768]{0,1:T(8,128)(2,1)}, u32[]{:S(2)}) copy-start(bf16[512,768]{0,1:T(8,128)(2,1)} %copy-done.19) | copy-start | bytes 2359300
  642.3 14.9 %all-to-all-start.6 = ((bf16[128,4,192]{0,2,1:T(8,128)(2,1)}), bf16[128,4,192]{0,2,1:T(8,128)(2,1)S(1)}, u32[]{:S(2)}, u32[]{:S(2)}) async-start(bf16[128,4,192]{0,2,1:T(8,128)(2,1)} %bitcast.84), calls=%async_computation.8 | async-start | bytes 393216 | tf_op jit(solution)/shard_map/all_to_all | solution.py:112
  657.2 8.6 all-to-all-start.7
  665.8 8.6 all-to-all-start.8
  669.2 67.2 %all-gather.23.cloned.1.call-start = ((), (), s32[]{:S(2)}) async-start(), calls=%async_computation.20 | async-start | bytes 7864320 | tf_op jit(solution)/shard_map/all_gather | solution.py:54
  677.2 11.9 %copy-start.43 = (f32[512,192]{0,1:T(8,128)S(1)}, f32[512,192]{0,1:T(8,128)}, u32[]{:S(2)}) copy-start(f32[512,192]{0,1:T(8,128)} %get-tuple-element.65) | copy-start | bytes 1179652
  691.2 108.7 %all-gather.25.cloned.1.call-start = ((), (), s32[]{:S(2)}) async-start(), calls=%async_computation.21 | async-start | bytes 7864320 | tf_op jit(solution)/shard_map/all_gather | solution.py:54
  753.5 127.1 %reduce-scatter.8.cloned.1.call-start = ((), (), s32[]{:S(2)}) async-start(), calls=%async_computation.22 | async-start | bytes 1310720 | tf_op jit(solution)/shard_map/reduce_scatter | solution.py:129
  811.6 10.9 %copy-start.72 = (f32[512]{0:T(512)S(1)}, f32[512]{0:T(512)}, u32[]{:S(2)}) copy-start(f32[512]{0:T(512)} %copy-done.70) | copy-start | bytes 6148
  811.6 10.9 %copy-start.81 = (f32[512]{0:T(512)S(1)}, f32[512]{0:T(512)}, u32[]{:S(2)}) copy-start(f32[512]{0:T(512)} %copy-done.80) | copy-start | bytes 6148
  822.5 10.7 %copy-start.24 = (bf16[512,768]{0,1:T(8,128)(2,1)S(1)}, bf16[512,768]{0,1:T(8,128)(2,1)}, u32[]{:S(2)}) copy-start(bf16[512,768]{0,1:T(8,128)(2,1)} %copy-done.22) | copy-start | bytes 2359300
  822.5 10.7 %copy-start.54 = (f32[768]{0:T(1024)S(1)}, f32[768]{0:T(1024)}, u32[]{:S(2)}) copy-start(f32[768]{0:T(1024)} %copy-done.52) | copy-start | bytes 9220
  851.3 29.3 %copy-start.34 = (bf16[128,1024]{1,0:T(8,128)(2,1)S(1)}, bf16[128,1024]{1,0:T(8,128)(2,1)}, u32[]{:S(2)}) copy-start(bf16[128,1024]{1,0:T(8,128)(2,1)} %bitcast_select_fusion) | copy-start | bytes 786436
  853.0 28.5 %copy-start.37 = (bf16[128,1024]{1,0:T(8,128)(2,1)S(1)}, bf16[128,1024]{1,0:T(8,128)(2,1)}, u32[]{:S(2)}) copy-start(bf16[128,1024]{1,0:T(8,128)(2,1)} %copy-done.36) | copy-start | bytes 786436
  853.0 28.5 %copy-start.39 = (bf16[128,1024]{1,0:T(8,128)(2,1)S(1)}, bf16[128,1024]{1,0:T(8,128)(2,1)}, u32[]{:S(2)}) copy-start(bf16[128,1024]{1,0:T(8,128)(2,1)} %copy-done.38) | copy-start | bytes 786436
  (67 other events, 353.1 us)
Sparse Core Ops, SparseCore 0:
  8.9 30.6 all-gather.26
  107.0 45.0 all-gather.10
  162.0 46.3 all-gather.12
  252.4 27.2 reduce-scatter.3
  291.8 27.8 all-gather.14
  392.8 45.0 all-gather.16
  454.7 46.3 all-gather.18
  551.6 27.2 reduce-scatter.5
  591.0 27.8 all-gather.20
  691.3 45.0 all-gather.22
  753.6 46.3 all-gather.24
  853.2 27.3 reduce-scatter.7
